TPU v7x, 32 devices: a whole 2x2x4 slice. The times are simulated.
32 devices in a mesh: expert: 16 (over z, y, x), dp: 2 (over core).
Axes of the slice: x: 2, y: 2, z: 4, core: 2. Of those that a mesh axis runs over, the one named last changes fastest.
Arguments:
- tokens: bfloat16 [2048, 2048], P(('expert', 'dp')), may hold values from -6 to 6
- expert_ids: int32 [2048, 8], P(('expert', 'dp')), may hold values from 0 to 15, all different within a row; in each aligned block of 64 rows (0 to 63, 64 to 127, ...) at most 48 rows name the same one
- gate_probs: float32 [2048, 8], P(('expert', 'dp')), may hold values from 0.05 to 1
- swap_flags: int32 [8], replicated, may hold values from 0 to 1, as said below
- w_gate: bfloat16 [16, 2048, 768], P('expert', 'dp'), may hold values from -0.125 to 0.125
- w_up: bfloat16 [16, 2048, 768], P('expert', 'dp'), may hold values from -0.125 to 0.125
- w_down: bfloat16 [16, 768, 2048], P('expert', None, 'dp'), may hold values from -0.21875 to 0.21875
Outputs:
- moe_out: bfloat16 [2048, 2048], P(('expert', 'dp'))
Inputs may be any that keep to these rules, and one draw needn't show every extreme that they name: `expert_ids`: each row names 8 different experts. Within the 64 rows of one device no expert is named by more than 48 rows, a bound that some block reaches. swap_flags[0] is 1; the other entries are 0 or 1.
All inputs are finite; a program needn't handle non-finite values.
Results may differ from a plain program's by a relative error of at most 0.0057.
Values may be sent and summed in bfloat16 or wider, within the bound.
A program may use at most 64 MiB of HBM per device.

v0:
```python
import jax
import jax.numpy as jnp
from jax import lax
from jax.sharding import PartitionSpec as P


def from_partner(shard, axis, distance):
    return lax.ppermute(shard, axis, [(i, i ^ 1 << distance) for i in range(lax.axis_size(axis))])


def on_device(tokens, expert_ids, gate_probs, swap_flags, w_gate, w_up, w_down):
    axis_size = lax.axis_size("expert")
    own_index = lax.axis_index("expert")
    half_span = axis_size // 2
    tok_count, top_count = expert_ids.shape
    model_width = tokens.shape[1]
    capacity = 3 * tok_count * top_count // (2 * axis_size)
    shares = gate_probs / jnp.sum(gate_probs, axis=1, keepdims=True)
    own_base = jnp.where(own_index < half_span, own_index, own_index - half_span)
    own_flag = (
        jnp.sum(jnp.where(jnp.arange(half_span, dtype=jnp.int32) == own_base, swap_flags, 0)) == 1
    )
    other_gate, other_up, other_down = from_partner(
        (w_gate, w_up, w_down), "expert", axis_size.bit_length() - 2
    )
    gate_block = jnp.where(own_flag, other_gate, w_gate)
    up_block = jnp.where(own_flag, other_up, w_up)
    down_block = jnp.where(own_flag, other_down, w_down)
    target_flat = expert_ids.reshape(-1)
    matches = (target_flat[:, None] == jnp.arange(axis_size, dtype=jnp.int32)[None, :]).astype(
        jnp.int32
    )
    before = jnp.cumsum(matches, axis=0) - matches
    position = jnp.sum(before * matches, axis=1)
    slot_index = target_flat * capacity + position
    source_rows = jnp.repeat(tokens, top_count, axis=0)
    outgoing = (
        jnp.zeros((axis_size * capacity, model_width), jnp.bfloat16).at[slot_index].set(source_rows)
    )
    arrived = lax.all_to_all(
        outgoing.reshape(axis_size, capacity, model_width),
        "expert",
        split_axis=0,
        concat_axis=0,
        tiled=True,
    )
    arrived_rows = arrived.reshape(axis_size * capacity, model_width)
    gate_next = jnp.dot(
        arrived_rows,
        lax.all_gather(gate_block, "dp", axis=1, tiled=True)[0],
        preferred_element_type=jnp.float32,
    )
    up_next = jnp.dot(
        arrived_rows,
        lax.all_gather(up_block, "dp", axis=1, tiled=True)[0],
        preferred_element_type=jnp.float32,
    )
    hidden = (jax.nn.silu(gate_next) * up_next).astype(jnp.bfloat16)
    produced = jnp.dot(
        hidden,
        lax.all_gather(down_block, "dp", axis=2, tiled=True)[0],
        preferred_element_type=jnp.float32,
    ).astype(jnp.bfloat16)
    returned = lax.all_to_all(
        produced.reshape(axis_size, capacity, model_width),
        "expert",
        split_axis=0,
        concat_axis=0,
        tiled=True,
    )
    picked = returned.reshape(axis_size * capacity, model_width)[slot_index]
    weighted = (
        picked.reshape(tok_count, top_count, model_width).astype(jnp.float32) * shares[:, :, None]
    )
    return jnp.sum(weighted, axis=1).astype(jnp.bfloat16)


def solution(mesh):
    placed = (
        P(("expert", "dp"), None),
        P(("expert", "dp"), None),
        P(("expert", "dp"), None),
        P(),
        P("expert", "dp", None),
        P("expert", "dp", None),
        P("expert", None, "dp"),
    )
    return jax.shard_map(
        on_device, mesh=mesh, in_specs=placed, out_specs=P(("expert", "dp"), None), check_vma=False
    )
```

profile of v0, /device:TPU:14, one launch (start us, length us, event | category | flops | bytes accessed | tf_op | source)
XLA Modules:
  0.0 402.4 jit_solution(16843100151016254630)
XLA Ops:
  6.5 2.6 collective-permute-start.1
  9.1 1.3 fusion.19
  11.1 65.6 %collective-permute-done.1 = bf16[1,1024,768]{2,1,0:T(8,128)(2,1)S(1)} collective-permute-done((bf16[1,1024,768]{2,1,0:T(8,128)(2,1)}, bf16[1,1024,768]{2,1,0:T(8,128)(2,1)S(1)}, u32[]{:S(2)}, u32[]{:S(2)}) %collective-permute-start.1) | collective-permute-done | bytes 1572896 | tf_op jit(solution)/shard_map/ppermute | solution.py:8
  76.7 2.8 broadcast_select_fusion.1
  79.5 0.0 all-gather.6.cloned.1.call-update
  79.5 3.3 collective-permute-start
  82.8 0.1 copy.10
  82.9 0.1 eq.38
  83.0 0.1 eq.34
  83.1 1.2 reduce-window.6
  84.3 0.2 slice_reduce_fusion
  84.5 0.1 copy.9
  84.6 0.1 mul.36
  84.7 0.1 fusion.17
  84.8 5.6 %scatter_custom_fusion = bf16[768,2048]{1,0:T(8,128)(2,1)} fusion(s32[512]{0:T(512)S(1)} %bitcast.50, bf16[]{:T(256)} %constant.7.clone.1, bf16[64,2048]{1,0:T(8,128)(2,1)S(1)} %copy-done), kind=kCustom, calls=%fused_computation.11 | custom fusion | bytes 3407874 | tf_op jit(solution)/shard_map/scatter | solution.py:38
  90.5 5.1 %all-to-all-start = ((bf16[16,48,2048]{2,1,0:T(8,128)(2,1)}), bf16[16,48,2048]{2,1,0:T(8,128)(2,1)S(1)}, u32[]{:S(2)}, u32[]{:S(2)}) async-start(bf16[16,48,2048]{2,1,0:T(8,128)(2,1)} %bitcast.4), calls=%async_computation | async-start | bytes 6291456 | tf_op jit(solution)/shard_map/all_to_all | solution.py:40
  95.6 0.0 all-gather.4.cloned.1.call-start
  95.6 84.1 %collective-permute-done = bf16[1,1024,768]{2,1,0:T(8,128)(2,1)} collective-permute-done((bf16[1,1024,768]{2,1,0:T(8,128)(2,1)}, bf16[1,1024,768]{2,1,0:T(8,128)(2,1)}, u32[]{:S(2)}, u32[]{:S(2)}) %collective-permute-start) | collective-permute-done | bytes 1572896 | tf_op jit(solution)/shard_map/ppermute | solution.py:8
  179.7 2.7 broadcast_select_fusion.2
  182.5 0.2 all-gather.8.cloned.1.call-start
  182.7 3.4 collective-permute-start.2
  186.2 94.6 %collective-permute-done.2 = bf16[1,768,1024]{2,1,0:T(8,128)(2,1)S(1)} collective-permute-done((bf16[1,768,1024]{2,1,0:T(8,128)(2,1)}, bf16[1,768,1024]{2,1,0:T(8,128)(2,1)S(1)}, u32[]{:S(2)}, u32[]{:S(2)}) %collective-permute-start.2) | collective-permute-done | bytes 1572896 | tf_op jit(solution)/shard_map/ppermute | solution.py:8
  280.8 2.8 broadcast_select_fusion
  283.6 0.0 all-gather.6.cloned.1.call-done
  283.6 5.9 %fusion.2 = f32[768,768]{1,0:T(8,128)} fusion(bf16[768,2048]{1,0:T(8,128)(2,1)S(1)} %bitcast.47, bf16[1,2048,768]{2,1,0:T(8,128)(2,1)} %all-gather.6.cloned.1.call-done), kind=kOutput, calls=%fused_computation.6 | convolution fusion | flops 2415919104 | bytes 8650752 | tf_op jit(solution)/shard_map/dot_general | solution.py:53
  289.5 8.4 %all-gather.8.cloned.1.call-done = bf16[1,768,2048]{2,1,0:T(8,128)(2,1)} async-done(((bf16[1,768,1024]{2,1,0:T(8,128)(2,1)}), bf16[1,768,2048]{2,1,0:T(8,128)(2,1)}) %all-gather.8.cloned.1.call-update) | async-done | bytes 3145744 | tf_op jit(solution)/shard_map/all_gather | solution.py:61
  297.9 11.0 %convolution_convert_fusion = bf16[768,2048]{1,0:T(8,128)(2,1)} fusion(bf16[1,768,2048]{2,1,0:T(8,128)(2,1)} %all-gather.8.cloned.1.call-done, f32[768,768]{1,0:T(8,128)} %fusion.2, bf16[768,2048]{1,0:T(8,128)(2,1)S(1)} %bitcast.48, bf16[1,2048,768]{2,1,0:T(8,128)(2,1)} %all-gather.4.cloned.1.call-done), kind=kOutput, calls=%fused_computation.4 | convolution fusion | flops 4836950016 | bytes 14942208 | tf_op jit(solution)/shard_map/dot_general | solution.py:59
  308.9 7.1 %all-to-all-start.1 = ((bf16[16,48,2048]{2,1,0:T(8,128)(2,1)}), bf16[16,48,2048]{2,1,0:T(8,128)(2,1)S(1)}, u32[]{:S(2)}, u32[]{:S(2)}) async-start(bf16[16,48,2048]{2,1,0:T(8,128)(2,1)} %bitcast.49), calls=%async_computation.1 | async-start | bytes 6291456 | tf_op jit(solution)/shard_map/all_to_all | solution.py:64
  316.0 0.1 copy.13
  316.1 72.2 %all-to-all-done.1 = bf16[16,48,2048]{2,1,0:T(8,128)(2,1)S(1)} async-done(((bf16[16,48,2048]{2,1,0:T(8,128)(2,1)}), bf16[16,48,2048]{2,1,0:T(8,128)(2,1)S(1)}, u32[]{:S(2)}, u32[]{:S(2)}) %all-to-all-start.1) | async-done | bytes 3145760 | tf_op jit(solution)/shard_map/all_to_all | solution.py:64
  388.3 3.3 gather_fusion
  391.7 4.1 %fusion = bf16[64,2048]{1,0:T(8,128)(2,1)} fusion(bf16[512,2048]{1,0:T(8,128)(2,1)} %gather_fusion, f32[64,8]{1,0:T(8,128)S(1)} %copy.13), kind=kLoop, calls=%fused_computation.3 | loop fusion | flops 3014656 | bytes 2361344 | tf_op jit(solution)/shard_map/reduce_sum | solution.py:75
  (19 shorter events, 0.1 us)
Async XLA Ops:
  6.5 78.3 %copy-start = (bf16[64,2048]{1,0:T(8,128)(2,1)S(1)}, bf16[64,2048]{1,0:T(8,128)(2,1)}, u32[]{:S(2)}) copy-start(bf16[64,2048]{1,0:T(8,128)(2,1)} %param.7) | copy-start | bytes 786436
  6.5 277.0 %all-gather.6.cloned.1.call-start = ((), (), s32[]{:S(2)}) async-start(), calls=%async_computation.3 | async-start | bytes 4718592 | tf_op jit(solution)/shard_map/all_gather | solution.py:55
  6.5 70.2 %collective-permute-start.1 = (bf16[1,1024,768]{2,1,0:T(8,128)(2,1)}, bf16[1,1024,768]{2,1,0:T(8,128)(2,1)S(1)}, u32[]{:S(2)}, u32[]{:S(2)}) collective-permute-start(bf16[1,1024,768]{2,1,0:T(8,128)(2,1)} %param.12), channel_id=1, source_target_pairs={{0,16},{2,18},{4,20},{6,22},{8,24},{10,26},{12,28},{14,30},{16,0},... | collective-permute-start | bytes 4718600 | tf_op jit(solution)/shard_map/ppermute | solution.py:8
  11.1 71.8 %copy-start.1 = (s32[64,8]{0,1:T(8,128)S(1)}, s32[64,8]{0,1:T(8,128)}, u32[]{:S(2)}) copy-start(s32[64,8]{0,1:T(8,128)} %param.8) | copy-start | bytes 6148
  79.5 100.3 %collective-permute-start = (bf16[1,1024,768]{2,1,0:T(8,128)(2,1)}, bf16[1,1024,768]{2,1,0:T(8,128)(2,1)}, u32[]{:S(2)}, u32[]{:S(2)}) collective-permute-start(bf16[1,1024,768]{2,1,0:T(8,128)(2,1)} %param.11), channel_id=1, source_target_pairs={{0,16},{2,18},{4,20},{6,22},{8,24},{10,26},{12,28},{14,30},{16,0},... | collective-permute-start | bytes 4718600 | tf_op jit(solution)/shard_map/ppermute | solution.py:8
  90.5 193.1 %all-to-all-start = ((bf16[16,48,2048]{2,1,0:T(8,128)(2,1)}), bf16[16,48,2048]{2,1,0:T(8,128)(2,1)S(1)}, u32[]{:S(2)}, u32[]{:S(2)}) async-start(bf16[16,48,2048]{2,1,0:T(8,128)(2,1)} %bitcast.4), calls=%async_computation | async-start | bytes 6291456 | tf_op jit(solution)/shard_map/all_to_all | solution.py:40
  95.6 193.9 %all-gather.4.cloned.1.call-start = ((), (), s32[]{:S(2)}) async-start(), calls=%async_computation.2 | async-start | bytes 4718592 | tf_op jit(solution)/shard_map/all_gather | solution.py:50
  182.5 115.4 %all-gather.8.cloned.1.call-start = ((), (), s32[]{:S(2)}) async-start(), calls=%async_computation.4 | async-start | bytes 4718592 | tf_op jit(solution)/shard_map/all_gather | solution.py:61
  182.7 98.1 %collective-permute-start.2 = (bf16[1,768,1024]{2,1,0:T(8,128)(2,1)}, bf16[1,768,1024]{2,1,0:T(8,128)(2,1)S(1)}, u32[]{:S(2)}, u32[]{:S(2)}) collective-permute-start(bf16[1,768,1024]{2,1,0:T(8,128)(2,1)} %param.13), channel_id=1, source_target_pairs={{0,16},{2,18},{4,20},{6,22},{8,24},{10,26},{12,28},{14,30},{16,0},... | collective-permute-start | bytes 4718600 | tf_op jit(solution)/shard_map/ppermute | solution.py:8
  308.9 7.1 %copy-start.2 = (f32[64,8]{0,1:T(8,128)S(1)}, f32[64,8]{0,1:T(8,128)}, u32[]{:S(2)}) copy-start(f32[64,8]{0,1:T(8,128)} %param.9) | copy-start | bytes 6148
  308.9 79.4 %all-to-all-start.1 = ((bf16[16,48,2048]{2,1,0:T(8,128)(2,1)}), bf16[16,48,2048]{2,1,0:T(8,128)(2,1)S(1)}, u32[]{:S(2)}, u32[]{:S(2)}) async-start(bf16[16,48,2048]{2,1,0:T(8,128)(2,1)} %bitcast.49), calls=%async_computation.1 | async-start | bytes 6291456 | tf_op jit(solution)/shard_map/all_to_all | solution.py:64
Sparse Core Ops, SparseCore 0:
  79.6 14.1 all-gather.5
  182.6 15.5 all-gather.3
  283.7 14.1 all-gather.7
where the time goes:
time: 403 us; the launch traced here: 402 us
  waiting for transfers between devices  325 us (81%)
  starting transfers between devices  21.8 us (5%)
  matrix products  16.9 us (4%)
  other arithmetic  15 us (4%)
  between operations  13.8 us (3%)
  local copies, waits for them, and re-layouts  9.75 us (2%)
    ppermute x3, waiting for transfers between devices, from_partner(): lax.ppermute(shard, axis, [(i, i ^ 1 << distance) for i in range(lax.axis...  244 us
    all_to_all x1, waiting for transfers between devices, on_device(): lax.all_to_all(produced.reshape(axis_size, capacity, model_width), 'exper...  72.2 us
    dot_general x1, matrix products, on_device(): jnp.dot(hidden, lax.all_gather(down_block, 'dp', axis=2, tiled=True)[0],...  11 us
    ppermute x3, starting transfers between devices, from_partner(): lax.ppermute(shard, axis, [(i, i ^ 1 << distance) for i in range(lax.axis...  9.38 us
    all_gather x1, waiting for transfers between devices, on_device(): lax.all_gather(down_block, 'dp', axis=2, tiled=True)[0]  8.37 us
  transfers between devices with their start and end apart: 8, of which 5 were waited for; matrix products, arithmetic and copies ran while one was open for 5% of the time, Pallas kernels for 0%

commit v1 on v0

v1 whole, which is shorter than its diff:
```python
import jax
import jax.numpy as jnp
from jax import lax
from jax.sharding import PartitionSpec as P


def on_device(tokens, expert_ids, gate_probs, swap_flags, w_gate, w_up, w_down):
    axis_size = lax.axis_size("expert")
    own_index = lax.axis_index("expert")
    half_span = axis_size // 2
    shares = gate_probs / jnp.sum(gate_probs, axis=1, keepdims=True)
    experts = jnp.arange(axis_size, dtype=jnp.int32)
    dense = jnp.sum(
        jnp.where(expert_ids[:, :, None] == experts[None, None, :], shares[:, :, None], 0.0), axis=1
    )
    lower = own_index < half_span
    own_base = jnp.where(lower, own_index, own_index - half_span)
    own_flag = (
        jnp.sum(jnp.where(jnp.arange(half_span, dtype=jnp.int32) == own_base, swap_flags, 0)) == 1
    )
    served = jnp.where(
        own_flag, jnp.where(lower, own_index + half_span, own_index - half_span), own_index
    )
    rows = lax.all_gather(tokens, "expert", axis=0, tiled=True)
    dense_all = lax.all_gather(dense, "expert", axis=0, tiled=True)
    factor = jnp.sum(jnp.where(experts[None, :] == served, dense_all, 0.0), axis=1)
    gate_next = jnp.dot(
        rows,
        lax.all_gather(w_gate, "dp", axis=1, tiled=True)[0],
        preferred_element_type=jnp.float32,
    )
    up_next = jnp.dot(
        rows,
        lax.all_gather(w_up, "dp", axis=1, tiled=True)[0],
        preferred_element_type=jnp.float32,
    )
    hidden = (jax.nn.silu(gate_next) * up_next).astype(jnp.bfloat16)
    produced = jnp.dot(
        hidden,
        lax.all_gather(w_down, "dp", axis=2, tiled=True)[0],
        preferred_element_type=jnp.float32,
    ).astype(jnp.bfloat16)
    partial = (factor[:, None] * produced.astype(jnp.float32)).astype(jnp.bfloat16)
    return lax.psum_scatter(partial, "expert", scatter_dimension=0, tiled=True)


def solution(mesh):
    placed = (
        P(("expert", "dp"), None),
        P(("expert", "dp"), None),
        P(("expert", "dp"), None),
        P(),
        P("expert", "dp", None),
        P("expert", "dp", None),
        P("expert", None, "dp"),
    )
    return jax.shard_map(
        on_device, mesh=mesh, in_specs=placed, out_specs=P(("expert", "dp"), None), check_vma=False
    )
```

time: 403 us -> 247 us (0.61)
  the two profiles are of different devices: /device:TPU:14 before, /device:TPU:0 now
where the time goes in v1:
time: 247 us
  waiting for transfers between devices  170 us (69%)
  blocking collectives  43.1 us (17%)
  matrix products  19 us (8%)
  between operations  13.9 us (6%)
    reduce_scatter x1, waiting for transfers between devices, on_device(): return lax.psum_scatter(partial, 'expert', scatter_dimension=0, tiled=True)  96.5 us
    all_gather x1, waiting for transfers between devices, on_device(): rows = lax.all_gather(tokens, 'expert', axis=0, tiled=True)  49.5 us
    all_gather x1, blocking collectives, on_device(): dense_all = lax.all_gather(dense, 'expert', axis=0, tiled=True)  43.1 us
    all_gather x1, waiting for transfers between devices, on_device(): lax.all_gather(w_down, 'dp', axis=2, tiled=True)[0]  14.7 us
    dot_general x1, matrix products, on_device(): jnp.dot(hidden, lax.all_gather(w_down, 'dp', axis=2, tiled=True)[0], pref...  12.8 us
    all_gather x1, waiting for transfers between devices, on_device(): lax.all_gather(w_gate, 'dp', axis=1, tiled=True)[0]  6.18 us
    dot_general x1, matrix products, on_device(): jnp.dot(rows, lax.all_gather(w_up, 'dp', axis=1, tiled=True)[0], preferre...  6.12 us
  transfers between devices with their start and end apart: 5, of which 4 were waited for; matrix products, arithmetic and copies ran while one was open for 3% of the time, Pallas kernels for 0%

profile of v1, /device:TPU:0, one launch (start us, length us, event | category | flops | bytes accessed | tf_op | source)
XLA Modules:
  0.0 246.6 jit_solution(10669585378727031929)
XLA Ops:
  6.5 0.0 copy-start
  6.5 0.0 copy-start.1
  6.5 0.0 copy-start.2
  6.5 0.0 all-gather.10.cloned.1.call-start
  6.5 0.7 all-gather.10.cloned.1.call-update
  7.3 0.0 all-gather.6.cloned.1.call-start
  7.3 0.7 all-gather.6.cloned.1.call-update
  8.0 0.0 all-gather.8.cloned.1.call-start
  8.1 0.7 all-gather.8.cloned.1.call-update
  8.7 0.0 all-gather.12.cloned.1.call-start
  8.8 0.5 all-gather.12.cloned.1.call-update
  9.3 0.0 reduce-scatter.2.cloned.1.call-start
  9.4 0.0 copy-done
  9.4 0.0 copy-done.1
  9.5 43.1 %all-gather = f32[16,64,16]{1,2,0:T(8,128)S(1)} all-gather(f32[1,64,16]{1,2,0:T(8,128)S(1)} %bitcast.18), channel_id=1, replica_groups=mesh['expert'=16,'dp'=2] {'expert'}, dimensions={0}, use_global_device_ids=true | all-gather | bytes 69632 | tf_op jit(solution)/shard_map/all_gather | solution.py:25
  52.6 0.1 reshape.10
  52.7 0.0 copy-done.2
  52.7 0.6 fusion.9
  54.0 0.1 select_reduce_fusion
  54.1 0.0 all-gather.10.cloned.1.call-done
  54.1 49.5 %all-gather.6.cloned.1.call-done = bf16[1024,2048]{1,0:T(8,128)(2,1)} async-done(((bf16[64,2048]{1,0:T(8,128)(2,1)}), bf16[1024,2048]{1,0:T(8,128)(2,1)}) %all-gather.6.cloned.1.call-update) | async-done | bytes 4194320 | tf_op jit(solution)/shard_map/all_gather | solution.py:24
  103.7 6.1 %fusion.1 = f32[1024,768]{1,0:T(8,128)S(1)} fusion(bf16[1024,2048]{1,0:T(8,128)(2,1)} %all-gather.6.cloned.1.call-done, bf16[1,2048,768]{2,1,0:T(8,128)(2,1)} %all-gather.10.cloned.1.call-done), kind=kOutput, calls=%fused_computation.2 | convolution fusion | flops 3221225472 | bytes 10485760 | tf_op jit(solution)/shard_map/dot_general | solution.py:32
  109.8 6.2 %all-gather.8.cloned.1.call-done = bf16[1,2048,768]{2,1,0:T(8,128)(2,1)} async-done(((bf16[1,1024,768]{2,1,0:T(8,128)(2,1)}), bf16[1,2048,768]{2,1,0:T(8,128)(2,1)}) %all-gather.8.cloned.1.call-update) | async-done | bytes 3145744 | tf_op jit(solution)/shard_map/all_gather | solution.py:29
  116.0 14.7 %all-gather.12.cloned.1.call-done = bf16[1,768,2048]{2,1,0:T(8,128)(2,1)} async-done(((bf16[1,768,1024]{2,1,0:T(8,128)(2,1)}), bf16[1,768,2048]{2,1,0:T(8,128)(2,1)}) %all-gather.12.cloned.1.call-update) | async-done | bytes 3145744 | tf_op jit(solution)/shard_map/all_gather | solution.py:40
  130.7 12.8 %multiply_convert_fusion = bf16[1024,2048]{1,0:T(8,128)(2,1)} fusion(f32[1024]{0:T(1024)S(1)} %select_reduce_fusion, bf16[1,768,2048]{2,1,0:T(8,128)(2,1)} %all-gather.12.cloned.1.call-done, f32[1024,768]{1,0:T(8,128)S(1)} %fusion.1, bf16[1024,2048]{1,0:T(8,128)(2,1)} %all-gather.6.cloned.1.call-done, bf16[1,2048,768]{2,1,0:T(8,128)(2,1)} %all-gather.8.cloned.1.call-done), kind=kOutput, calls=%fused_computation | convolution fusion | flops 6455558144 | bytes 17829888 | tf_op jit(solution)/shard_map/dot_general | solution.py:38
  143.5 0.0 reduce-scatter.2.cloned.1.call-update
  143.6 96.5 %reduce-scatter.2.cloned.1.call-done = bf16[64,2048]{1,0:T(8,128)(2,1)} async-done(((bf16[1024,2048]{1,0:T(8,128)(2,1)}), bf16[64,2048]{1,0:T(8,128)(2,1)}) %reduce-scatter.2.cloned.1.call-update) | async-done | bytes 262160 | tf_op jit(solution)/shard_map/reduce_scatter | solution.py:44
  (5 shorter events, 0.1 us)
Async XLA Ops:
  6.5 2.8 %copy-start = (f32[64,8]{0,1:T(8,128)S(1)}, f32[64,8]{0,1:T(8,128)}, u32[]{:S(2)}) copy-start(f32[64,8]{0,1:T(8,128)} %param.9) | copy-start | bytes 6148
  6.5 2.9 %copy-start.1 = (s32[64,8]{0,1:T(8,128)S(1)}, s32[64,8]{0,1:T(8,128)}, u32[]{:S(2)}) copy-start(s32[64,8]{0,1:T(8,128)} %param.8) | copy-start | bytes 6148
  6.5 46.2 %copy-start.2 = (s32[8]{0:T(128)S(1)}, s32[8]{0:T(128)}, u32[]{:S(2)}) copy-start(s32[8]{0:T(128)} %param.10) | copy-start | bytes 100
  6.5 47.6 %all-gather.10.cloned.1.call-start = ((), (), s32[]{:S(2)}) async-start(), calls=%async_computation.3 | async-start | bytes 4718592 | tf_op jit(solution)/shard_map/all_gather | solution.py:34
  7.3 96.4 %all-gather.6.cloned.1.call-start = ((), (), s32[]{:S(2)}) async-start(), calls=%async_computation.1 | async-start | bytes 4456448 | tf_op jit(solution)/shard_map/all_gather | solution.py:24
  8.0 108.0 %all-gather.8.cloned.1.call-start = ((), (), s32[]{:S(2)}) async-start(), calls=%async_computation.2 | async-start | bytes 4718592 | tf_op jit(solution)/shard_map/all_gather | solution.py:29
  8.7 121.9 %all-gather.12.cloned.1.call-start = ((), (), s32[]{:S(2)}) async-start(), calls=%async_computation.4 | async-start | bytes 4718592 | tf_op jit(solution)/shard_map/all_gather | solution.py:40
  9.3 230.7 %reduce-scatter.2.cloned.1.call-start = ((), (), s32[]{:S(2)}) async-start(), calls=%async_computation.5 | async-start | bytes 4456448 | tf_op jit(solution)/shard_map/reduce_scatter | solution.py:44
Sparse Core Ops, SparseCore 0:
  8.9 14.8 all-gather.9
  26.5 77.0 all-gather.5
  105.2 10.7 all-gather.7
  117.4 13.2 all-gather.11
  143.7 96.3 reduce-scatter.1

commit v2 on v1

--- a/solution.py
+++ b/solution.py
@@ -1,7 +1,336 @@
+import functools
+
 import jax
 import jax.numpy as jnp
 from jax import lax
+from jax.experimental import pallas as pl
+from jax.experimental.pallas import tpu as pltpu
 from jax.sharding import PartitionSpec as P
+
+MESH = pl.DeviceIdType.MESH
+
+
+def flipped(index, bit):
+    return index + bit * (1 - 2 * lax.rem(lax.div(index, bit), 2))
+
+
+def slot_of(mask, deep):
+    return (mask % 4) * deep + mask // 4
+
+
+def level_of(mask, order):
+    return max([i for i, bit in enumerate(order) if mask & bit], default=-1)
+
+
+def fused_kernel(
+    n,
+    flags_ref,
+    ids_ref,
+    probs_ref,
+    tokens_ref,
+    gate_ref,
+    up_ref,
+    down_ref,
+    out_ref,
+    rows_buf,
+    gate_buf,
+    up_buf,
+    down_buf,
+    table_buf,
+    hidden_buf,
+    total_buf,
+    leave_buf,
+    land_buf,
+    weight_sems,
+    peer_send,
+    peer_recv,
+    own_sems,
+    row_send,
+    row_recv,
+    table_send,
+    table_recv,
+    sum_send,
+    sum_recv,
+):
+    me = lax.axis_index("expert")
+    core = lax.axis_index("dp")
+    top, count = ids_ref.shape
+    width = rows_buf.shape[-1]
+    hid = hidden_buf.shape[1]
+    deep = n // 4
+    line = [1 << i for i in range(2, n.bit_length() - 1)]
+    orders = (line + [1, 2], line + [2, 1])
+    bits = line + [1, 2]
+    target = {bit: {"expert": flipped(me, bit)} for bit in bits}
+    peer = {"dp": 1 - core}
+
+    barrier = pltpu.get_barrier_semaphore()
+    for device in [target[bit] for bit in bits] + [peer]:
+        pl.semaphore_signal(barrier, inc=1, device_id=device, device_id_type=MESH)
+
+    own_weights = [
+        pltpu.make_async_copy(src.at[0], dst.at[core], weight_sems.at[i])
+        for i, (src, dst) in enumerate(
+            ((gate_ref, gate_buf), (up_ref, up_buf), (down_ref, down_buf))
+        )
+    ]
+    own_rows = [
+        pltpu.make_async_copy(
+            tokens_ref.at[:, pl.ds(half * width, width)], rows_buf.at[half, 0], own_sems.at[half]
+        )
+        for half in range(2)
+    ]
+    for copy in own_rows + own_weights:
+        copy.start()
+
+    probs = probs_ref[...]
+    shares = probs / jnp.sum(probs, axis=0, keepdims=True)
+    row = lax.broadcasted_iota(jnp.int32, (n, count), 0)
+    base = jnp.where(row < n // 2, row, row - n // 2)
+    flag = jnp.zeros((n, count), jnp.int32)
+    for j in range(n // 2):
+        flag = jnp.where(base == j, flags_ref[j], flag)
+    other = jnp.where(row < n // 2, row + n // 2, row - n // 2)
+    served = jnp.where(flag == 1, other, row)
+    table = jnp.zeros((n, count), jnp.float32)
+    for k in range(top):
+        table = table + jnp.where(ids_ref[k : k + 1, :] == served, shares[k : k + 1, :], 0.0)
+    table_buf[0] = table
+
+    pl.semaphore_wait(barrier, len(bits) + 1)
+
+    def row_copy(half, mask, bit):
+        there = mask ^ bit
+        slot = slot_of(there, deep)
+        src = rows_buf.at[half, slot_of(mask, deep)]
+        if mask == 0:
+            src = tokens_ref.at[:, pl.ds(half * width, width)]
+        return pltpu.make_async_remote_copy(
+            src_ref=src,
+            dst_ref=rows_buf.at[half, slot],
+            send_sem=row_send.at[half, slot],
+            recv_sem=row_recv.at[half, slot],
+            device_id=target[bit],
+            device_id_type=MESH,
+        )
+
+    def table_copy(mask, bit):
+        slot = slot_of(mask ^ bit, deep)
+        return pltpu.make_async_remote_copy(
+            src_ref=table_buf.at[slot_of(mask, deep)],
+            dst_ref=table_buf.at[slot],
+            send_sem=table_send.at[slot],
+            recv_sem=table_recv.at[slot],
+            device_id=target[bit],
+            device_id_type=MESH,
+        )
+
+    sent = []
+
+    def start(copy):
+        copy.start()
+        sent.append(copy)
+
+    def arrival(half, mask):
+        bit = orders[half][level_of(mask, orders[half])]
+        return row_copy(half, mask ^ bit, bit)
+
+    arrived = set()
+
+    def take(half, mask):
+        if mask == 0 or (half, mask) in arrived:
+            return
+        arrived.add((half, mask))
+        order = orders[half]
+        level = level_of(mask, order)
+        arrival(half, mask).wait_recv()
+        if half == 0:
+            table_copy(mask ^ order[level], order[level]).wait_recv()
+        for bit in order[level + 1 :]:
+            if half == 0:
+                start(table_copy(mask, bit))
+            start(row_copy(half, mask, bit))
+
+    for bit in bits:
+        start(table_copy(0, bit))
+    for bit in line:
+        for half in range(2):
+            start(row_copy(half, 0, bit))
+        if bit == line[0]:
+            start(row_copy(0, 0, 1))
+            start(row_copy(1, 0, 2))
+    peer_weights = []
+    for i, (src, dst) in enumerate(((gate_ref, gate_buf), (up_ref, up_buf), (down_ref, down_buf))):
+        copy = pltpu.make_async_remote_copy(
+            src_ref=src.at[0],
+            dst_ref=dst.at[core],
+            send_sem=peer_send.at[i],
+            recv_sem=peer_recv.at[i],
+            device_id=peer,
+            device_id_type=MESH,
+        )
+        copy.start()
+        peer_weights.append(copy)
+    start(row_copy(0, 0, 2))
+    start(row_copy(1, 0, 1))
+
+    def sum_copy(half, mask):
+        order = orders[half]
+        bit = order[level_of(mask, order)]
+        slot = slot_of(mask, deep)
+        return pltpu.make_async_remote_copy(
+            src_ref=leave_buf.at[half, slot],
+            dst_ref=land_buf.at[half, slot],
+            send_sem=sum_send.at[half, slot],
+            recv_sem=sum_recv.at[half, slot],
+            device_id=target[bit],
+            device_id_type=MESH,
+        )
+
+    square_row = lax.broadcasted_iota(jnp.int32, (count, count), 0)
+    square_column = lax.broadcasted_iota(jnp.int32, (count, count), 1)
+
+    def factor_of(slot):
+        mine = jnp.sum(jnp.where(row == me, table_buf[slot], 0.0), axis=0, keepdims=True)
+        return jnp.sum(jnp.where(square_row == square_column, mine, 0.0), axis=1, keepdims=True)
+
+    tile = 256
+
+    def compute(batch):
+        first = batch * deep
+        chunk = deep * count
+
+        def hidden_step(j, carry):
+            columns = pl.ds(pl.multiple_of(j * tile, tile), tile)
+            gate = jnp.zeros((chunk, tile), jnp.float32)
+            up = jnp.zeros((chunk, tile), jnp.float32)
+            for half in range(2):
+                x = rows_buf[half, first : first + deep].reshape(chunk, width)
+                gate = gate + jnp.dot(
+                    x, gate_buf[half, :, columns], preferred_element_type=jnp.float32
+                )
+                up = up + jnp.dot(x, up_buf[half, :, columns], preferred_element_type=jnp.float32)
+            silu = gate / (1.0 + jnp.exp(-gate))
+            hidden_buf[:, columns] = (silu * up).astype(jnp.bfloat16)
+            return carry
+
+        lax.fori_loop(0, hid // tile, hidden_step, 0)
+        factors = jnp.concatenate([factor_of(first + i) for i in range(deep)], axis=0)
+        halves = (1, 0) if batch == 1 else (0, 1)
+        for half in halves:
+            final = level_of(batch, orders[half]) == len(bits) - 1
+
+            def down_step(j, carry, half=half, final=final):
+                columns = pl.ds(pl.multiple_of(j * tile, tile), tile)
+                made = jnp.dot(
+                    hidden_buf[...],
+                    down_buf[half, :, columns],
+                    preferred_element_type=jnp.float32,
+                ).astype(jnp.bfloat16)
+                part = made.astype(jnp.float32) * factors
+                for i in range(deep):
+                    block = part[i * count : (i + 1) * count]
+                    if final:
+                        leave_buf[half, first + i, :, columns] = block.astype(jnp.bfloat16)
+                    else:
+                        total_buf[half, first + i, :, columns] = block
+                return carry
+
+            lax.fori_loop(0, width // tile, down_step, 0)
+            if final:
+                for high in range(deep - 1, -1, -1):
+                    start(sum_copy(half, high * 4 + batch))
+
+    highs = list(range(deep))
+    for high in highs[1:]:
+        for half in range(2):
+            take(half, high * 4)
+        take(0, (high - 1) * 4 + 1)
+        take(1, (high - 1) * 4 + 2)
+    for copy in own_rows + own_weights:
+        copy.wait()
+    for copy in peer_weights:
+        copy.wait_recv()
+    take(0, highs[-1] * 4 + 1)
+    take(1, highs[-1] * 4 + 2)
+    compute(0)
+    for batch in (1, 2, 3):
+        for high in highs:
+            for half in range(2):
+                take(half, high * 4 + batch)
+        compute(batch)
+
+    def gathered(half, mask):
+        order = orders[half]
+        total = total_buf[half, slot_of(mask, deep)]
+        for bit in reversed(order[level_of(mask, order) + 1 :]):
+            sum_copy(half, mask ^ bit).wait_recv()
+            total = total + land_buf[half, slot_of(mask ^ bit, deep)].astype(jnp.float32)
+        return total
+
+    for high in reversed(highs):
+        for half in range(2):
+            mask = high * 4 + orders[half][-2]
+            leave_buf[half, slot_of(mask, deep)] = gathered(half, mask).astype(jnp.bfloat16)
+            start(sum_copy(half, mask))
+    for high in reversed(highs):
+        for half in range(2):
+            mask = high * 4
+            if mask:
+                leave_buf[half, slot_of(mask, deep)] = gathered(half, mask).astype(jnp.bfloat16)
+                start(sum_copy(half, mask))
+            else:
+                out_ref[:, half * width : (half + 1) * width] = gathered(half, 0).astype(
+                    jnp.bfloat16
+                )
+    for copy in sent + peer_weights:
+        copy.wait_send()
+
+
+def in_one_kernel(tokens, expert_ids, gate_probs, swap_flags, w_gate, w_up, w_down):
+    n = lax.axis_size("expert")
+    count, model = tokens.shape
+    width = model // 2
+    hid = w_gate.shape[2]
+    deep = n // 4
+    any_spec = pl.BlockSpec(memory_space=pl.ANY)
+    vmem_spec = pl.BlockSpec(memory_space=pltpu.VMEM)
+    dma = pltpu.SemaphoreType.DMA
+    return pl.pallas_call(
+        functools.partial(fused_kernel, n),
+        out_shape=jax.ShapeDtypeStruct((count, model), jnp.bfloat16),
+        in_specs=[pl.BlockSpec(memory_space=pltpu.SMEM), vmem_spec, vmem_spec] + [any_spec] * 4,
+        out_specs=vmem_spec,
+        scratch_shapes=[
+            pltpu.VMEM((2, n, count, width), jnp.bfloat16),
+            pltpu.VMEM((2, width, hid), jnp.bfloat16),
+            pltpu.VMEM((2, width, hid), jnp.bfloat16),
+            pltpu.VMEM((2, hid, width), jnp.bfloat16),
+            pltpu.VMEM((n, n, count), jnp.float32),
+            pltpu.VMEM((deep * count, hid), jnp.bfloat16),
+            pltpu.VMEM((2, n, count, width), jnp.float32),
+            pltpu.VMEM((2, n, count, width), jnp.bfloat16),
+            pltpu.VMEM((2, n, count, width), jnp.bfloat16),
+            dma((3,)),
+            dma((3,)),
+            dma((3,)),
+            dma((2,)),
+            dma((2, n)),
+            dma((2, n)),
+            dma((n,)),
+            dma((n,)),
+            dma((2, n)),
+            dma((2, n)),
+        ],
+        compiler_params=pltpu.CompilerParams(
+            collective_id=0, has_side_effects=True, vmem_limit_bytes=48 << 20
+        ),
+    )(swap_flags, expert_ids.T, gate_probs.T, tokens, w_gate, w_up, w_down)
+
+
+def kernel_fits(mesh):
+    n = mesh.shape["expert"]
+    return mesh.shape["dp"] == 2 and n in (8, 16)
 
 
 def on_device(tokens, expert_ids, gate_probs, swap_flags, w_gate, w_up, w_down):
@@ -55,5 +384,6 @@
         P("expert", None, "dp"),
     )
     return jax.shard_map(
-        on_device, mesh=mesh, in_specs=placed, out_specs=P(("expert", "dp"), None), check_vma=False
-    )
+        in_one_kernel if kernel_fits(mesh) else on_device,
+        mesh=mesh, in_specs=placed, out_specs=P(("expert", "dp"), None), check_vma=False
+    )

time: 247 us -> 105 us (0.43)
  waiting for transfers between devices: 170 us -> 0 us
  Pallas kernels: 0 us -> 97.2 us
  blocking collectives: 43.1 us -> 0 us
  matrix products: 19 us -> 0 us
  between operations: 13.9 us -> 0.02 us
  local copies, waits for them, and re-layouts: 0.15 us -> 7.9 us
    pallas_call x0 -> x1, Pallas kernels: none -> 97.2 us  [in_one_kernel(): pl.pallas_call(functools.partial(fused_kernel, n), out_shape=jax.ShapeDty...]
    reduce_scatter x1 -> x0, waiting for transfers between devices: 96.5 us -> none  [on_device(): return lax.psum_scatter(partial, 'expert', scatter_dimension=0, tiled=True)]
    all_gather x4 -> x0, waiting for transfers between devices: 70.5 us -> none  [the longest x1 49.5 us: on_device(): rows = lax.all_gather(tokens, 'expert', axis=0, tiled=True)]
    all_gather x1 -> x0, blocking collectives: 43.1 us -> none  [on_device(): dense_all = lax.all_gather(dense, 'expert', axis=0, tiled=True)]
    dot_general x2 -> x0, matrix products: 19 us -> none  [the longest x1 12.8 us: on_device(): jnp.dot(hidden, lax.all_gather(w_down, 'dp', axis=2, tiled=True)[0], pref...]
    unnamed x7 -> x15, local copies, waits for them, and re-layouts: 0.11 us -> 7.9 us
    unnamed x5 -> x0, waiting for transfers between devices: 2.63 us -> none
  transfers between devices with their start and end apart: 5 -> 0, of which waited for: 4 -> 0; matrix products, arithmetic and copies ran while one was open for 3% -> 0% of each run, Pallas kernels for 0% -> 0%
where the time goes in v2:
time: 105 us
  Pallas kernels  97.2 us (93%)
  local copies, waits for them, and re-layouts  7.9 us (8%)
    pallas_call x1, Pallas kernels, in_one_kernel(): pl.pallas_call(functools.partial(fused_kernel, n), out_shape=jax.ShapeDty...  97.2 us
    unnamed x15, local copies, waits for them, and re-layouts  7.9 us

profile of v2, /device:TPU:0, one launch (start us, length us, event | category | flops | bytes accessed | tf_op | source)
XLA Modules:
  0.0 105.1 jit_solution(14292053229335770840)
XLA Ops:
  0.0 0.0 copy-start
  0.0 1.4 %copy-done = bf16[1,1024,768]{2,1,0:T(8,128)(2,1)S(1)} copy-done((bf16[1,1024,768]{2,1,0:T(8,128)(2,1)S(1)}, bf16[1,1024,768]{2,1,0:T(8,128)(2,1)}, u32[]{:S(2)}) %copy-start) | copy-done | bytes 1572888
  1.4 0.0 copy-start.1
  1.4 1.4 %copy-done.1 = bf16[1,1024,768]{2,1,0:T(8,128)(2,1)S(1)} copy-done((bf16[1,1024,768]{2,1,0:T(8,128)(2,1)S(1)}, bf16[1,1024,768]{2,1,0:T(8,128)(2,1)}, u32[]{:S(2)}) %copy-start.1) | copy-done | bytes 1572888
  2.8 0.0 copy-start.2
  2.8 1.4 %copy-done.2 = bf16[1,768,1024]{2,1,0:T(8,128)(2,1)S(1)} copy-done((bf16[1,768,1024]{2,1,0:T(8,128)(2,1)S(1)}, bf16[1,768,1024]{2,1,0:T(8,128)(2,1)}, u32[]{:S(2)}) %copy-start.2) | copy-done | bytes 1572888
  4.2 0.0 copy-start.3
  4.2 0.9 copy-done.3
  5.2 0.0 copy-start.4
  5.2 0.7 copy-done.4
  5.9 0.0 copy-start.5
  5.9 0.7 copy-done.5
  6.6 0.0 copy-start.6
  6.6 0.7 copy-done.6
  7.2 97.2 %shard_map.73 = bf16[64,2048]{1,0:T(8,128)(2,1)S(1)} custom-call(s32[8]{0:T(128)S(1)} %copy-done.6, s32[8,64]{1,0:T(8,128)S(1)} %bitcast.2, f32[8,64]{1,0:T(8,128)S(1)} %bitcast.3, bf16[64,2048]{1,0:T(8,128)(2,1)S(1)} %copy-done.3, bf16[1,1024,768]{2,1,0:T(8,128)(2,1)S(1)} %copy-done, bf16[1,1024,768]{2,1,0:T(8,128)(2,1)S(1)} %copy-done.1, ...), custom_call_target="tpu_custom_call" | custom-call | tf_op jit(solution)/shard_map/pallas_call | solution.py:299
  104.4 0.7 copy.9
Async XLA Ops:
  0.0 1.4 %copy-start = (bf16[1,1024,768]{2,1,0:T(8,128)(2,1)S(1)}, bf16[1,1024,768]{2,1,0:T(8,128)(2,1)}, u32[]{:S(2)}) copy-start(bf16[1,1024,768]{2,1,0:T(8,128)(2,1)} %gate_ref.1) | copy-start | bytes 4718596
  1.4 1.4 %copy-start.1 = (bf16[1,1024,768]{2,1,0:T(8,128)(2,1)S(1)}, bf16[1,1024,768]{2,1,0:T(8,128)(2,1)}, u32[]{:S(2)}) copy-start(bf16[1,1024,768]{2,1,0:T(8,128)(2,1)} %up_ref.1) | copy-start | bytes 4718596
  2.8 1.4 %copy-start.2 = (bf16[1,768,1024]{2,1,0:T(8,128)(2,1)S(1)}, bf16[1,768,1024]{2,1,0:T(8,128)(2,1)}, u32[]{:S(2)}) copy-start(bf16[1,768,1024]{2,1,0:T(8,128)(2,1)} %down_ref.1) | copy-start | bytes 4718596
  4.2 0.9 copy-start.3
  5.2 0.7 copy-start.4
  5.9 0.7 copy-start.5
  6.6 0.7 copy-start.6

commit v3 on v2

--- a/solution.py
+++ b/solution.py
@@ -58,7 +58,7 @@
     width = rows_buf.shape[-1]
     hid = hidden_buf.shape[1]
     deep = n // 4
-    line = [1 << i for i in range(2, n.bit_length() - 1)]
+    line = [1 << i for i in reversed(range(2, n.bit_length() - 1))]
     orders = (line + [1, 2], line + [2, 1])
     bits = line + [1, 2]
     target = {bit: {"expert": flipped(me, bit)} for bit in bits}
@@ -153,12 +153,11 @@
 
     for bit in bits:
         start(table_copy(0, bit))
-    for bit in line:
-        for half in range(2):
-            start(row_copy(half, 0, bit))
-        if bit == line[0]:
-            start(row_copy(0, 0, 1))
-            start(row_copy(1, 0, 2))
+    near, far = line[-1], line[:-1]
+    start(row_copy(0, 0, near))
+    start(row_copy(0, 0, 1))
+    start(row_copy(1, 0, 2))
+    start(row_copy(1, 0, near))
     peer_weights = []
     for i, (src, dst) in enumerate(((gate_ref, gate_buf), (up_ref, up_buf), (down_ref, down_buf))):
         copy = pltpu.make_async_remote_copy(
@@ -171,8 +170,6 @@
         )
         copy.start()
         peer_weights.append(copy)
-    start(row_copy(0, 0, 2))
-    start(row_copy(1, 0, 1))
 
     def sum_copy(half, mask):
         order = orders[half]
@@ -195,6 +192,7 @@
         return jnp.sum(jnp.where(square_row == square_column, mine, 0.0), axis=1, keepdims=True)
 
     tile = 256
+    highs = list(range(deep))
 
     def compute(batch):
         first = batch * deep
@@ -237,28 +235,6 @@
                 return carry
 
             lax.fori_loop(0, width // tile, down_step, 0)
-            if final:
-                for high in range(deep - 1, -1, -1):
-                    start(sum_copy(half, high * 4 + batch))
-
-    highs = list(range(deep))
-    for high in highs[1:]:
-        for half in range(2):
-            take(half, high * 4)
-        take(0, (high - 1) * 4 + 1)
-        take(1, (high - 1) * 4 + 2)
-    for copy in own_rows + own_weights:
-        copy.wait()
-    for copy in peer_weights:
-        copy.wait_recv()
-    take(0, highs[-1] * 4 + 1)
-    take(1, highs[-1] * 4 + 2)
-    compute(0)
-    for batch in (1, 2, 3):
-        for high in highs:
-            for half in range(2):
-                take(half, high * 4 + batch)
-        compute(batch)
 
     def gathered(half, mask):
         order = orders[half]
@@ -268,21 +244,74 @@
             total = total + land_buf[half, slot_of(mask ^ bit, deep)].astype(jnp.float32)
         return total
 
-    for high in reversed(highs):
+    def leave(half, mask):
+        leave_buf[half, slot_of(mask, deep)] = gathered(half, mask).astype(jnp.bfloat16)
+        start(sum_copy(half, mask))
+
+    def take_pair(high):
+        take(0, high * 4 + 1)
+        take(1, high * 4 + 2)
+
+    take_pair(0)
+    take(0, near)
+    start(row_copy(1, 0, 1))
+    start(row_copy(0, 0, 2))
+    take(1, near)
+    for bit in far:
         for half in range(2):
-            mask = high * 4 + orders[half][-2]
-            leave_buf[half, slot_of(mask, deep)] = gathered(half, mask).astype(jnp.bfloat16)
-            start(sum_copy(half, mask))
-    for high in reversed(highs):
+            start(row_copy(half, 0, bit))
+    line_order = [near // 4] + [high for high in highs[1:] if high != near // 4]
+    for last, high in zip([0] + line_order, line_order):
+        take(0, high * 4)
+        take(1, high * 4)
+        if last:
+            take_pair(last)
+    for copy in own_rows + own_weights:
+        copy.wait()
+    for copy in peer_weights:
+        copy.wait_recv()
+    compute(0)
+    take_pair(line_order[-1])
+    for batch in (1, 2):
+        for high in highs:
+            for half in range(2):
+                take(half, high * 4 + batch)
+        compute(batch)
+        half = 2 - batch
+        for high in reversed(highs):
+            start(sum_copy(half, high * 4 + batch))
+    for high in highs:
         for half in range(2):
-            mask = high * 4
-            if mask:
-                leave_buf[half, slot_of(mask, deep)] = gathered(half, mask).astype(jnp.bfloat16)
-                start(sum_copy(half, mask))
+            take(half, high * 4 + 3)
+    compute(3)
+
+    back = list(reversed(highs))
+
+    def corner(high):
+        for half in range(2):
+            start(sum_copy(half, high * 4 + 3))
+
+    def side(high):
+        for half in range(2):
+            leave(half, high * 4 + orders[half][-2])
+
+    def stem(high):
+        for half in range(2):
+            if high:
+                leave(half, high * 4)
             else:
                 out_ref[:, half * width : (half + 1) * width] = gathered(half, 0).astype(
                     jnp.bfloat16
                 )
+
+    lead = 2
+    for step in range(deep + lead + 2):
+        if step < deep:
+            corner(back[step])
+        if 0 <= step - lead + 1 < deep:
+            side(back[step - lead + 1])
+        if 0 <= step - lead < deep:
+            stem(back[step - lead])
     for copy in sent + peer_weights:
         copy.wait_send()
 
@@ -293,7 +322,7 @@
     width = model // 2
     hid = w_gate.shape[2]
     deep = n // 4
-    any_spec = pl.BlockSpec(memory_space=pl.ANY)
+    any_spec = pl.BlockSpec(memory_space=pltpu.HBM)
     vmem_spec = pl.BlockSpec(memory_space=pltpu.VMEM)
     dma = pltpu.SemaphoreType.DMA
     return pl.pallas_call(
@@ -323,7 +352,7 @@
             dma((2, n)),
         ],
         compiler_params=pltpu.CompilerParams(
-            collective_id=0, has_side_effects=True, vmem_limit_bytes=48 << 20
+            collective_id=0, has_side_effects=True, vmem_limit_bytes=60 << 20
         ),
     )(swap_flags, expert_ids.T, gate_probs.T, tokens, w_gate, w_up, w_down)
 

time: 105 us -> 90 us (0.86)
  Pallas kernels: 97.2 us -> 88.1 us
  local copies, waits for them, and re-layouts: 7.9 us -> 1.67 us
    pallas_call x1, Pallas kernels: 97.2 us -> 88.1 us  [in_one_kernel(): pl.pallas_call(functools.partial(fused_kernel, n), out_shape=jax.ShapeDty...]
    unnamed x15 -> x1, local copies, waits for them, and re-layouts: 7.9 us -> 1.67 us
where the time goes in v3:
time: 90 us; the launch traced here: 89.8 us
  Pallas kernels  88.1 us (98%)
  local copies, waits for them, and re-layouts  1.67 us (2%)
    pallas_call x1, Pallas kernels, in_one_kernel(): pl.pallas_call(functools.partial(fused_kernel, n), out_shape=jax.ShapeDty...  88.1 us

profile of v3, /device:TPU:0, one launch (start us, length us, event | category | flops | bytes accessed | tf_op | source)
XLA Modules:
  0.0 89.8 jit_solution(15255999880363328560)
XLA Ops:
  0.0 88.1 %shard_map.73 = bf16[64,2048]{1,0:T(8,128)(2,1)} custom-call(s32[8]{0:T(128)} %flags_ref.1, s32[8,64]{1,0:T(8,128)} %bitcast.2, f32[8,64]{1,0:T(8,128)} %bitcast.3, bf16[64,2048]{1,0:T(8,128)(2,1)} %tokens_ref.1, bf16[1,1024,768]{2,1,0:T(8,128)(2,1)} %gate_ref.1, bf16[1,1024,768]{2,1,0:T(8,128)(2,1)} %up_ref.1, bf16[1,768,1024]{2,1,0:T(8,128)(2,1)} %down_ref.1), custom_call_target="tpu_custom_call" | custom-call | tf_op jit(solution)/shard_map/pallas_call | solution.py:328
  88.1 1.7 %copy.9 = bf16[64,2048]{1,0:T(8,128)(2,1)} copy(bf16[64,2048]{1,0:T(8,128)(2,1)} %shard_map.73) | data formatting | bytes 524288

commit v4 on v3

--- a/solution.py
+++ b/solution.py
@@ -158,6 +158,7 @@
     start(row_copy(0, 0, 1))
     start(row_copy(1, 0, 2))
     start(row_copy(1, 0, near))
+    start(row_copy(0, 0, far[0]))
     peer_weights = []
     for i, (src, dst) in enumerate(((gate_ref, gate_buf), (up_ref, up_buf), (down_ref, down_buf))):
         copy = pltpu.make_async_remote_copy(
@@ -257,9 +258,7 @@
     start(row_copy(1, 0, 1))
     start(row_copy(0, 0, 2))
     take(1, near)
-    for bit in far:
-        for half in range(2):
-            start(row_copy(half, 0, bit))
+    start(row_copy(1, 0, far[0]))
     line_order = [near // 4] + [high for high in highs[1:] if high != near // 4]
     for last, high in zip([0] + line_order, line_order):
         take(0, high * 4)
@@ -278,7 +277,7 @@
                 take(half, high * 4 + batch)
         compute(batch)
         half = 2 - batch
-        for high in reversed(highs):
+        for high in list(reversed(highs))[:2]:
             start(sum_copy(half, high * 4 + batch))
     for high in highs:
         for half in range(2):
@@ -310,6 +309,9 @@
             corner(back[step])
         if 0 <= step - lead + 1 < deep:
             side(back[step - lead + 1])
+        if 2 <= step + 1 < deep:
+            for half in range(2):
+                start(sum_copy(half, back[step + 1] * 4 + orders[half][-1]))
         if 0 <= step - lead < deep:
             stem(back[step - lead])
     for copy in sent + peer_weights:

time: 90 us -> 89.1 us (0.990)
  no operation moved by 1% of the time
where the time goes in v4:
time: 89.1 us; the launch traced here: 88.9 us
  Pallas kernels  87.3 us (98%)
  local copies, waits for them, and re-layouts  1.67 us (2%)
    pallas_call x1, Pallas kernels, in_one_kernel(): pl.pallas_call(functools.partial(fused_kernel, n), out_shape=jax.ShapeDty...  87.3 us

profile of v4, /device:TPU:0, one launch (start us, length us, event | category | flops | bytes accessed | tf_op | source)
XLA Modules:
  0.0 88.9 jit_solution(7536247191377561437)
XLA Ops:
  0.0 87.3 %shard_map.73 = bf16[64,2048]{1,0:T(8,128)(2,1)} custom-call(s32[8]{0:T(128)} %flags_ref.1, s32[8,64]{1,0:T(8,128)} %bitcast.2, f32[8,64]{1,0:T(8,128)} %bitcast.3, bf16[64,2048]{1,0:T(8,128)(2,1)} %tokens_ref.1, bf16[1,1024,768]{2,1,0:T(8,128)(2,1)} %gate_ref.1, bf16[1,1024,768]{2,1,0:T(8,128)(2,1)} %up_ref.1, bf16[1,768,1024]{2,1,0:T(8,128)(2,1)} %down_ref.1), custom_call_target="tpu_custom_call" | custom-call | tf_op jit(solution)/shard_map/pallas_call | solution.py:330
  87.3 1.7 %copy.9 = bf16[64,2048]{1,0:T(8,128)(2,1)} copy(bf16[64,2048]{1,0:T(8,128)(2,1)} %shard_map.73) | data formatting | bytes 524288
